TPU v7x, 32 devices: a whole 2x2x4 slice. The times are simulated.
32 devices in a mesh: grp: 4 (over x, core), dev: 8 (over z, y).
Axes of the slice: x: 2, y: 2, z: 4, core: 2. Of those that a mesh axis runs over, the one named last changes fastest.
Arguments:
- coefficients: float32 [2, 8, 64, 4096], P(None, None, None, ('grp', 'dev')), may hold values from -6 to 6
- spatial_root: int32 [64], replicated, may hold values from 0 to 1023
- frequency_root: int32 [64], replicated, may hold values from 0 to 255
Outputs:
- result: float32 [2, 8, 64, 4096], P(None, None, None, ('grp', 'dev'))
All inputs are finite; a program needn't handle non-finite values.
Results may differ from a plain program's by a relative error of at most 0.002.
Values sent between devices are 32-bit elements; how exact they have to be, the bound alone decides.
A program may use at most 64 MiB of HBM per device.

v0:
```python
import math
import jax
import jax.numpy as jnp
from jax import lax
from jax.sharding import PartitionSpec as P

LEVELS = 12
HIGHEST = lax.Precision.HIGHEST


def partner_2(block, axis, distance):
    count = lax.axis_size(axis)
    route = []
    for low in range(count):
        high = low | 1 << distance
        if high != low and high < count:
            route += [(low, high), (high, low)]
    return lax.ppermute(block, axis, route)


def cheb_nodes():
    node_order = jnp.arange(8, dtype=jnp.float32)
    return 0.5 - 0.5 * jnp.cos(math.pi * (2.0 * node_order + 1.0) / 16.0)


def lagrange_table(half_cell):
    points = cheb_nodes()
    target = (points + half_cell) / 2.0
    diagonal = jnp.arange(8)[:, None] == jnp.arange(8)[None, :]
    numerator = jnp.where(
        diagonal[None, :, :], jnp.float32(1.0), target[:, None, None] - points[None, None, :]
    )
    denominator = jnp.where(diagonal, jnp.float32(1.0), points[:, None] - points[None, :])
    return jnp.prod(numerator, axis=2) / jnp.prod(denominator, axis=1)[None, :]


def interp_tables():
    halves = [lagrange_table(0.0), lagrange_table(1.0)]
    return jnp.stack(
        [jnp.kron(halves[quadrant % 2], halves[quadrant // 2]) for quadrant in range(4)]
    )


def pair_digits(pair_index, pairs_dev, devices_dev):
    quarter = pairs_dev // 4
    within = pair_index % pairs_dev
    device = pair_index // pairs_dev % devices_dev
    group_id = pair_index // (pairs_dev * devices_dev)
    places = [device % 4, group_id % 4, within // quarter]
    return (places, device // 4 * quarter + within % quarter)


def pair_boxes(pair_index, level_step, box_roots, pairs_dev, devices_dev, levels):
    places, _ = pair_digits(pair_index, pairs_dev, devices_dev)
    coarse_space = levels // 2 - 1
    coarse_wave = levels // 2 - 2
    space_row = box_roots[0] // 2**coarse_space
    space_column = box_roots[0] % 2**coarse_space
    for position in range(level_step):
        space_row = 2 * space_row + places[position] % 2
        space_column = 2 * space_column + places[position] // 2
    wave_row = box_roots[1] // 2**coarse_wave
    wave_column = box_roots[1] % 2**coarse_wave
    for position in range(2, level_step - 1, -1):
        wave_row = 2 * wave_row + places[position] % 2
        wave_column = 2 * wave_column + places[position] // 2
    space_side = 0.5 ** (coarse_space + level_step)
    wave_side = float(2**levels) / float(2 ** (coarse_wave + 3 - level_step))
    offset = -0.5 * float(2**levels)
    space_box = (
        space_row.astype(jnp.float32) * space_side,
        space_column.astype(jnp.float32) * space_side,
        space_side,
    )
    wave_box = (
        offset + wave_row.astype(jnp.float32) * wave_side,
        offset + wave_column.astype(jnp.float32) * wave_side,
        wave_side,
    )
    return (space_box, wave_box)


def box_points(square):
    points = cheb_nodes()
    first_axis = jnp.repeat(points, 8)
    second_axis = jnp.tile(points, 8)
    return (
        square[0][None, :] + square[2] * first_axis[:, None],
        square[1][None, :] + square[2] * second_axis[:, None],
    )


def box_center(square):
    return (square[0] + 0.5 * square[2], square[1] + 0.5 * square[2])


def phase_angle(first_space, second_space, first_wave, second_wave):
    two_pi = 2.0 * math.pi
    wave_speed = 16.0 * math.pi
    speed_one = (
        2.0 + jnp.sin(wave_speed * first_space) * jnp.sin(wave_speed * second_space)
    ) / 16.0
    speed_two = (
        2.0 + jnp.cos(wave_speed * first_space) * jnp.cos(wave_speed * second_space)
    ) / 16.0
    radial = jnp.sqrt(
        speed_one * speed_one * first_wave * first_wave
        + speed_two * speed_two * second_wave * second_wave
    )
    return two_pi * (first_space * first_wave + second_space * second_wave + radial)


def rotate(values, turn_angle):
    cosine = jnp.cos(turn_angle)
    sine_part = jnp.sin(turn_angle)
    return jnp.stack(
        [values[0] * cosine - values[1] * sine_part, values[0] * sine_part + values[1] * cosine]
    )


def pre_merge(
    children, new_index, new_roots, child_index, child_roots, pairs_dev, devices_dev, levels
):
    space_box, wave_box = pair_boxes(new_index, 1, new_roots, pairs_dev, devices_dev, levels)
    center_one, center_two = box_center(space_box)
    turned = []
    for child_id in range(4):
        _, child_wave = pair_boxes(
            child_index[child_id],
            0,
            (child_roots[0][child_id], child_roots[1][child_id]),
            pairs_dev,
            devices_dev,
            levels,
        )
        wave_one, wave_two = box_points(child_wave)
        turned.append(
            rotate(
                children[child_id],
                -phase_angle(center_one[None, :], center_two[None, :], wave_one, wave_two),
            )
        )
    summed = jnp.einsum("cst,caksm->aktm", interp_tables(), jnp.stack(turned), precision=HIGHEST)
    wave_one, wave_two = box_points(wave_box)
    return rotate(summed, phase_angle(center_one[None, :], center_two[None, :], wave_one, wave_two))


def switch_step(values, pair_index, box_roots, pairs_dev, devices_dev, levels):
    space_box, wave_box = pair_boxes(pair_index, 1, box_roots, pairs_dev, devices_dev, levels)
    space_one, space_two = box_points(space_box)
    wave_one, wave_two = box_points(wave_box)
    kernel_angle = phase_angle(
        space_one[:, None, :], space_two[:, None, :], wave_one[None, :, :], wave_two[None, :, :]
    )
    cosine = jnp.cos(kernel_angle)
    sine_part = jnp.sin(kernel_angle)
    real_part = jnp.einsum("tsm,ksm->ktm", cosine, values[0], precision=HIGHEST) - jnp.einsum(
        "tsm,ksm->ktm", sine_part, values[1], precision=HIGHEST
    )
    imag_part = jnp.einsum("tsm,ksm->ktm", sine_part, values[0], precision=HIGHEST) + jnp.einsum(
        "tsm,ksm->ktm", cosine, values[1], precision=HIGHEST
    )
    return jnp.stack([real_part, imag_part]) / 64.0


def post_terms(values, pair_index, box_roots, level_step, pairs_dev, devices_dev, levels):
    space_box, wave_box = pair_boxes(
        pair_index, level_step, box_roots, pairs_dev, devices_dev, levels
    )
    space_one, space_two = box_points(space_box)
    center_one, center_two = box_center(wave_box)
    return rotate(
        values, -phase_angle(space_one, space_two, center_one[None, :], center_two[None, :])
    )


def post_finish(merged, pair_index, box_roots, level_step, pairs_dev, devices_dev, levels):
    space_box, wave_box = pair_boxes(
        pair_index, level_step, box_roots, pairs_dev, devices_dev, levels
    )
    space_one, space_two = box_points(space_box)
    center_one, center_two = box_center(wave_box)
    return rotate(
        merged, phase_angle(space_one, space_two, center_one[None, :], center_two[None, :])
    )


def lookup_roots(pair_index, spatial_root, frequency_root, pairs_dev, devices_dev):
    _, block_id = pair_digits(pair_index, pairs_dev, devices_dev)
    matches = block_id[..., None] == jnp.arange(spatial_root.shape[0], dtype=jnp.int32)
    return (
        jnp.sum(jnp.where(matches, spatial_root, 0), axis=-1),
        jnp.sum(jnp.where(matches, frequency_root, 0), axis=-1),
    )


def middle_levels(first_level, held_index, held_roots, group_id, pairs_dev, devices_dev, total_fn):
    switched = switch_step(first_level, held_index, held_roots, pairs_dev, devices_dev, LEVELS)
    child_terms = post_terms(switched, held_index, held_roots, 1, pairs_dev, devices_dev, LEVELS)
    summed = total_fn(child_terms)
    local_interp = lax.dynamic_index_in_dim(interp_tables(), group_id, 0, keepdims=False)
    spread_level = jnp.einsum("ts,aksm->aktm", local_interp, summed, precision=HIGHEST)
    return post_finish(spread_level, held_index, held_roots, 2, pairs_dev, devices_dev, LEVELS)


def per_device(coefficients, spatial_root, frequency_root):
    rhs_count = coefficients.shape[1]
    rank_count = coefficients.shape[2]
    pairs_dev = coefficients.shape[3]
    devices_dev = lax.axis_size("dev")
    group_id = lax.axis_index("grp")
    device_id = lax.axis_index("dev")
    base_index = group_id * (devices_dev * pairs_dev)
    own_index = base_index + device_id * pairs_dev + jnp.arange(pairs_dev, dtype=jnp.int32)
    own_roots = lookup_roots(own_index, spatial_root, frequency_root, pairs_dev, devices_dev)
    stacked = coefficients[None]
    for bit_number in range(2):
        partner = partner_2(stacked, "dev", bit_number)
        upper_half = device_id // 2**bit_number % 2
        stacked = jnp.where(
            upper_half == 1,
            jnp.concatenate([partner, stacked]),
            jnp.concatenate([stacked, partner]),
        )
    child_index = (
        own_index[None, :] + (jnp.arange(4, dtype=jnp.int32)[:, None] - device_id % 4) * pairs_dev
    )
    child_roots = lookup_roots(child_index, spatial_root, frequency_root, pairs_dev, devices_dev)
    first_level = pre_merge(
        stacked, own_index, own_roots, child_index, child_roots, pairs_dev, devices_dev, LEVELS
    )
    second = middle_levels(
        first_level,
        own_index,
        own_roots,
        group_id,
        pairs_dev,
        devices_dev,
        lambda terms: lax.psum(terms, "grp"),
    )
    child_terms = post_terms(second, own_index, own_roots, 2, pairs_dev, devices_dev, LEVELS)
    summed = jnp.sum(child_terms.reshape(2, rhs_count, rank_count, 4, pairs_dev // 4), axis=3)
    spread_last = jnp.einsum("jts,aksm->aktjm", interp_tables(), summed, precision=HIGHEST).reshape(
        2, rhs_count, rank_count, pairs_dev
    )
    return post_finish(spread_last, own_index, own_roots, 3, pairs_dev, devices_dev, LEVELS)


def solution(mesh):
    return jax.shard_map(
        per_device,
        mesh=mesh,
        in_specs=(P(None, None, None, ("grp", "dev")), P(), P()),
        out_specs=P(None, None, None, ("grp", "dev")),
        check_vma=False,
    )
```

profile of v0, /device:TPU:0, one launch (start us, length us, event | category | flops | bytes accessed | tf_op | source)
XLA Modules:
  0.0 217.6 jit_solution(8685077930100766251)
XLA Ops:
  6.5 3.0 %collective-permute-start = (f32[1,2,8,64,128]{4,3,2,1,0:T(8,128)}, f32[1,2,8,64,128]{4,3,2,1,0:T(8,128)S(1)}, u32[]{:S(2)}, u32[]{:S(2)}) collective-permute-start(f32[1,2,8,64,128]{4,3,2,1,0:T(8,128)} %bitcast.157), channel_id=1, source_target_pairs={{0,1},{1,0},{2,3},{3,2},{4,5},{5,4},{6,7},{7,6},{8,9},{9,8},{10,11... | collective-permute-start | bytes 1572872 | tf_op jit(solution)/shard_map/ppermute | solution.py:18
  9.8 0.8 select_reduce_fusion.4
  10.7 0.1 broadcast_add_fusion.4
  10.8 0.8 select_reduce_fusion
  11.6 0.2 select_reduce_fusion.5
  11.8 0.3 select_reduce_fusion.2
  12.2 0.1 add_bitcast_fusion.7
  12.4 0.1 copy.54
  12.5 0.1 mul.2649
  12.7 0.1 mul.2645
  12.8 0.5 fusion.152
  13.3 0.1 broadcast_multiply_fusion.1
  13.4 8.3 %collective-permute-done = f32[1,2,8,64,128]{4,3,2,1,0:T(8,128)S(1)} collective-permute-done((f32[1,2,8,64,128]{4,3,2,1,0:T(8,128)}, f32[1,2,8,64,128]{4,3,2,1,0:T(8,128)S(1)}, u32[]{:S(2)}, u32[]{:S(2)}) %collective-permute-start) | collective-permute-done | bytes 524320 | tf_op jit(solution)/shard_map/ppermute | solution.py:18
  21.7 1.4 maximum_select_fusion.1
  23.1 1.9 collective-permute-start.1
  25.0 0.1 mul.2633
  25.2 0.1 mul.2628
  25.3 0.1 mul.2528
  25.4 0.1 mul.2519
  25.5 0.1 mul.2615
  25.6 0.1 mul.2618
  25.8 0.1 mul.2621
  25.9 0.1 mul.2623
  26.0 0.1 copy.61
  26.1 0.1 copy.60
  26.2 0.8 fusion.150
  27.0 0.1 copy.59
  27.1 0.1 copy.58
  27.2 0.1 copy.57
  27.3 0.1 copy.56
  27.4 0.1 copy.67
  27.5 0.1 copy.66
  27.7 0.1 mul.2729
  27.8 0.1 mul.2723
  28.0 0.5 fusion.140
  28.4 19.0 %collective-permute-done.1 = f32[2,2,8,64,128]{4,3,2,1,0:T(8,128)S(1)} collective-permute-done((f32[2,2,8,64,128]{4,3,2,1,0:T(8,128)S(1)}, f32[2,2,8,64,128]{4,3,2,1,0:T(8,128)S(1)}, u32[]{:S(2)}, u32[]{:S(2)}) %collective-permute-start.1) | collective-permute-done | bytes 1048608 | tf_op jit(solution)/shard_map/ppermute | solution.py:18
  47.5 0.3 maximum_select_fusion
  47.8 0.2 multiply_subtract_fusion.8
  48.1 0.1 multiply_subtract_fusion.7
  48.3 1.5 fusion.46
  49.8 0.2 copy.63
  50.1 0.2 copy.62
  50.3 29.0 %fusion.2 = f32[128,8,64]{2,1,0:T(8,128)S(1)} fusion(f32[8,64,128]{1,0,2:T(8,128)S(1)} %copy.63, f32[64,128]{0,1:T(8,128)S(1)} %copy.61, f32[64,128]{0,1:T(8,128)S(1)} %copy.60, f32[64,128]{0,1:T(8,128)S(1)} %copy.59, f32[64,128]{0,1:T(8,128)S(1)} %copy.58, f32[64,128]{0,1:T(8,128)S(1)} %copy.57, f32[64,128]{0,1:T(8,128)S(1)} %copy.56), kind=kOutput, calls=%fused_computation.3 | convolution fusion | flops 55574528 | bytes 720896 | tf_op jit(solution)/shard_map/tsm,ksm->ktm/dot_general | solution.py:160
  79.3 28.8 %fusion.4 = f32[128,8,64]{2,1,0:T(8,128)S(1)} fusion(f32[8,64,128]{1,0,2:T(8,128)S(1)} %copy.62, f32[64,128]{0,1:T(8,128)S(1)} %copy.61, f32[64,128]{0,1:T(8,128)S(1)} %copy.60, f32[64,128]{0,1:T(8,128)S(1)} %copy.59, f32[64,128]{0,1:T(8,128)S(1)} %copy.58, f32[64,128]{0,1:T(8,128)S(1)} %copy.57, f32[64,128]{0,1:T(8,128)S(1)} %copy.56), kind=kOutput, calls=%fused_computation.4 | convolution fusion | flops 55574528 | bytes 720896 | tf_op jit(solution)/shard_map/tsm,ksm->ktm/dot_general | solution.py:157
  108.1 29.0 %fusion.58 = f32[1,8,64,128]{2,1,3,0:T(8,128)S(1)} fusion(f32[128,8,64]{2,1,0:T(8,128)S(1)} %fusion.2, f32[8,64,128]{1,0,2:T(8,128)S(1)} %copy.62, f32[64,128]{0,1:T(8,128)S(1)} %copy.61, f32[64,128]{0,1:T(8,128)S(1)} %copy.60, f32[64,128]{0,1:T(8,128)S(1)} %copy.59, f32[64,128]{0,1:T(8,128)S(1)} %copy.58, f32[64,128]{0,1:T(8,128)S(1)} %copy.57, ...), kind=kOutput, calls=%fused_computation.50 | convolution fusion | flops 55640064 | bytes 983040 | tf_op jit(solution)/shard_map/tsm,ksm->ktm/dot_general | solution.py:160
  137.1 29.0 %fusion.52 = f32[1,8,64,128]{2,1,3,0:T(8,128)S(1)} fusion(f32[128,8,64]{2,1,0:T(8,128)S(1)} %fusion.4, f32[8,64,128]{1,0,2:T(8,128)S(1)} %copy.63, f32[64,128]{0,1:T(8,128)S(1)} %copy.61, f32[64,128]{0,1:T(8,128)S(1)} %copy.60, f32[64,128]{0,1:T(8,128)S(1)} %copy.59, f32[64,128]{0,1:T(8,128)S(1)} %copy.58, f32[64,128]{0,1:T(8,128)S(1)} %copy.57, ...), kind=kOutput, calls=%fused_computation.48 | convolution fusion | flops 55640064 | bytes 983040 | tf_op jit(solution)/shard_map/tsm,ksm->ktm/dot_general | solution.py:157
  166.1 0.1 maximum_multiply_fusion
  166.2 0.1 multiply_subtract_fusion
  166.3 1.1 pad_maximum_fusion
  167.5 0.1 mul.2693
  167.6 0.1 mul.2687
  167.7 0.6 fusion.138
  168.3 36.7 %all-reduce.2.cloned.1.call-done = f32[2,8,64,128]{2,1,3,0:T(8,128)} async-done(((f32[2,8,64,128]{2,1,3,0:T(8,128)}), f32[2,8,64,128]{2,1,3,0:T(8,128)}) %all-reduce.2.cloned.1.call-update) | async-done | bytes 524304 | tf_op jit(solution)/shard_map/psum | solution.py:239
  205.1 2.6 %convolution_bitcast_fusion.1 = f32[2,8,64,128]{3,2,1,0:T(8,128)S(1)} fusion(f32[2,8,64,128]{2,1,3,0:T(8,128)} %all-reduce.2.cloned.1.call-done, f32[4,64,64]{1,2,0:T(8,128)S(1)} %constant_dynamic-update-slice_fusion, s32[]{:T(128)S(6)} %select_n.1084), kind=kOutput, calls=%fused_computation.46 | convolution fusion | flops 100663296 | bytes 1081348 | tf_op jit(solution)/shard_map/ts,aksm->aktm/dot_general | solution.py:202
  207.7 0.1 multiply_subtract_fusion.2
  207.8 0.2 copy.71
  208.0 0.2 copy.70
  208.2 0.1 maximum_reduce_fusion
  208.3 1.0 convolution_bitcast_fusion
  209.3 0.1 fusion.207
  209.4 0.2 copy.74
  209.6 0.2 copy.73
  209.8 0.1 multiply_subtract_fusion.1
  209.9 0.8 pad_maximum_fusion.1
  (42 shorter events, 1.3 us)
Async XLA Ops:
  6.5 198.5 %all-reduce.2.cloned.1.call-start = ((), (), s32[]{:S(2)}) async-start(), calls=%async_computation | async-start | bytes 2097152 | tf_op jit(solution)/shard_map/psum | solution.py:239
  6.5 15.1 %collective-permute-start = (f32[1,2,8,64,128]{4,3,2,1,0:T(8,128)}, f32[1,2,8,64,128]{4,3,2,1,0:T(8,128)S(1)}, u32[]{:S(2)}, u32[]{:S(2)}) collective-permute-start(f32[1,2,8,64,128]{4,3,2,1,0:T(8,128)} %bitcast.157), channel_id=1, source_target_pairs={{0,1},{1,0},{2,3},{3,2},{4,5},{5,4},{6,7},{7,6},{8,9},{9,8},{10,11... | collective-permute-start | bytes 1572872 | tf_op jit(solution)/shard_map/ppermute | solution.py:18
  23.1 24.4 %collective-permute-start.1 = (f32[2,2,8,64,128]{4,3,2,1,0:T(8,128)S(1)}, f32[2,2,8,64,128]{4,3,2,1,0:T(8,128)S(1)}, u32[]{:S(2)}, u32[]{:S(2)}) collective-permute-start(f32[2,2,8,64,128]{4,3,2,1,0:T(8,128)S(1)} %maximum_select_fusion.1), channel_id=1, source_target_pairs={{0,2},{2,0},{1,3},{3,1},{4,6},{6,4},{5,7},{7,5},{8,10},{10,8},{9,1... | collective-permute-start | bytes 3145736 | tf_op jit(solution)/shard_map/ppermute | solution.py:18
Sparse Core Ops, SparseCore 0:
  167.6 37.4 all-reduce.1
where the time goes:
time: 218 us
  matrix products  121 us (56%)
  waiting for transfers between devices  64 us (29%)
  between operations  14 us (6%)
  other arithmetic  10 us (5%)
  starting transfers between devices  4.86 us (2%)
  local copies, waits for them, and re-layouts  3.9 us (2%)
    psum x1, waiting for transfers between devices, per_device(): lax.psum(terms, 'grp')  36.7 us
    dot_general x1, matrix products, switch_step(): jnp.einsum('tsm,ksm->ktm', cosine, values[1], precision=HIGHEST)  29 us
    dot_general x1, matrix products, switch_step(): jnp.einsum('tsm,ksm->ktm', sine_part, values[0], precision=HIGHEST)  29 us
    dot_general x1, matrix products, switch_step(): jnp.einsum('tsm,ksm->ktm', sine_part, values[1], precision=HIGHEST)  29 us
    dot_general x1, matrix products, switch_step(): jnp.einsum('tsm,ksm->ktm', cosine, values[0], precision=HIGHEST)  28.8 us
    ppermute x2, waiting for transfers between devices, partner_2(): return lax.ppermute(block, axis, route)  27.3 us
    ppermute x2, starting transfers between devices, partner_2(): return lax.ppermute(block, axis, route)  4.86 us
  transfers between devices with their start and end apart: 3, of which 3 were waited for; matrix products, arithmetic and copies ran while one was open for 4% of the time, Pallas kernels for 0%

commit v1 on v0

--- a/solution.py
+++ b/solution.py
@@ -236,7 +236,7 @@
         group_id,
         pairs_dev,
         devices_dev,
-        lambda terms: lax.psum(terms, "grp"),
+        lambda terms: jnp.sum(lax.all_gather(terms, "grp"), axis=0),
     )
     child_terms = post_terms(second, own_index, own_roots, 2, pairs_dev, devices_dev, LEVELS)
     summed = jnp.sum(child_terms.reshape(2, rhs_count, rank_count, 4, pairs_dev // 4), axis=3)

time: 218 us -> 203 us (0.931)
  waiting for transfers between devices: 64 us -> 51.1 us
    psum x1 -> x0, waiting for transfers between devices: 36.7 us -> none  [per_device(): lax.psum(terms, 'grp')]
    all_gather x0 -> x1, waiting for transfers between devices: none -> 22.1 us  [per_device(): lax.all_gather(terms, 'grp')]
where the time goes in v1:
time: 203 us; the launch traced here: 202 us
  matrix products  119 us (59%)
  waiting for transfers between devices  51.1 us (25%)
  between operations  14 us (7%)
  other arithmetic  8.82 us (4%)
  local copies, waits for them, and re-layouts  5.04 us (2%)
  starting transfers between devices  4.8 us (2%)
    dot_general x1, matrix products, switch_step(): jnp.einsum('tsm,ksm->ktm', cosine, values[1], precision=HIGHEST)  29 us
    dot_general x1, matrix products, switch_step(): jnp.einsum('tsm,ksm->ktm', sine_part, values[0], precision=HIGHEST)  29 us
    dot_general x1, matrix products, switch_step(): jnp.einsum('tsm,ksm->ktm', sine_part, values[1], precision=HIGHEST)  29 us
    ppermute x2, waiting for transfers between devices, partner_2(): return lax.ppermute(block, axis, route)  28.9 us
    dot_general x1, matrix products, switch_step(): jnp.einsum('tsm,ksm->ktm', cosine, values[0], precision=HIGHEST)  28.8 us
    all_gather x1, waiting for transfers between devices, per_device(): lax.all_gather(terms, 'grp')  22.1 us
    ppermute x2, starting transfers between devices, partner_2(): return lax.ppermute(block, axis, route)  4.79 us
  transfers between devices with their start and end apart: 3, of which 3 were waited for; matrix products, arithmetic and copies ran while one was open for 4% of the time, Pallas kernels for 0%

profile of v1, /device:TPU:0, one launch (start us, length us, event | category | flops | bytes accessed | tf_op | source)
XLA Modules:
  0.0 202.5 jit_solution(16782362663185226382)
XLA Ops:
  6.5 3.0 %collective-permute-start = (f32[1,2,8,64,128]{4,3,2,1,0:T(8,128)}, f32[1,2,8,64,128]{4,3,2,1,0:T(8,128)S(1)}, u32[]{:S(2)}, u32[]{:S(2)}) collective-permute-start(f32[1,2,8,64,128]{4,3,2,1,0:T(8,128)} %bitcast.160), channel_id=1, source_target_pairs={{0,1},{1,0},{2,3},{3,2},{4,5},{5,4},{6,7},{7,6},{8,9},{9,8},{10,11... | collective-permute-start | bytes 1572872 | tf_op jit(solution)/shard_map/ppermute | solution.py:18
  9.9 0.8 select_reduce_fusion.4
  10.8 0.1 mul.2633
  10.9 0.1 mul.2628
  11.0 0.1 mul.2528
  11.2 0.1 mul.2519
  11.3 0.2 select_reduce_fusion.5
  11.5 0.3 select_reduce_fusion.2
  12.0 0.1 broadcast_multiply_fusion.1
  12.1 0.1 mul.2615
  12.2 0.1 mul.2618
  12.4 0.1 mul.2621
  12.5 0.1 mul.2623
  12.6 0.1 mul.2649
  12.8 0.1 mul.2645
  12.9 0.5 fusion.151
  13.4 0.1 copy.85
  13.5 0.1 copy.84
  13.6 0.1 broadcast_add_fusion.4
  13.7 0.1 select_reduce_fusion
  13.9 0.1 add_bitcast_fusion.7
  14.0 7.8 %collective-permute-done = f32[1,2,8,64,128]{4,3,2,1,0:T(8,128)S(1)} collective-permute-done((f32[1,2,8,64,128]{4,3,2,1,0:T(8,128)}, f32[1,2,8,64,128]{4,3,2,1,0:T(8,128)S(1)}, u32[]{:S(2)}, u32[]{:S(2)}) %collective-permute-start) | collective-permute-done | bytes 524320 | tf_op jit(solution)/shard_map/ppermute | solution.py:18
  21.7 0.1 maximum_select_fusion.1
  21.9 1.8 collective-permute-start.1
  23.7 0.8 fusion.149
  24.5 0.1 copy.83
  24.6 0.1 copy.82
  24.7 0.1 copy.81
  24.8 0.1 copy.80
  24.9 0.1 copy.91
  25.0 0.1 copy.90
  25.1 21.1 %collective-permute-done.1 = f32[2,2,8,64,128]{4,3,2,1,0:T(8,128)S(1)} collective-permute-done((f32[2,2,8,64,128]{4,3,2,1,0:T(8,128)S(1)}, f32[2,2,8,64,128]{4,3,2,1,0:T(8,128)S(1)}, u32[]{:S(2)}, u32[]{:S(2)}) %collective-permute-start.1) | collective-permute-done | bytes 1048608 | tf_op jit(solution)/shard_map/ppermute | solution.py:18
  46.2 0.3 maximum_select_fusion
  46.5 0.2 multiply_subtract_fusion.8
  46.9 0.1 multiply_subtract_fusion.7
  47.0 1.5 fusion.46
  48.6 0.2 copy.87
  48.9 0.2 copy.86
  49.1 29.0 %fusion.2 = f32[128,8,64]{2,1,0:T(8,128)S(1)} fusion(f32[8,64,128]{1,0,2:T(8,128)S(1)} %copy.87, f32[64,128]{0,1:T(8,128)S(1)} %copy.85, f32[64,128]{0,1:T(8,128)S(1)} %copy.84, f32[64,128]{0,1:T(8,128)S(1)} %copy.83, f32[64,128]{0,1:T(8,128)S(1)} %copy.82, f32[64,128]{0,1:T(8,128)S(1)} %copy.81, f32[64,128]{0,1:T(8,128)S(1)} %copy.80), kind=kOutput, calls=%fused_computation.3 | convolution fusion | flops 55574528 | bytes 720896 | tf_op jit(solution)/shard_map/tsm,ksm->ktm/dot_general | solution.py:160
  78.1 28.8 %fusion.4 = f32[128,8,64]{2,1,0:T(8,128)S(1)} fusion(f32[8,64,128]{1,0,2:T(8,128)S(1)} %copy.86, f32[64,128]{0,1:T(8,128)S(1)} %copy.85, f32[64,128]{0,1:T(8,128)S(1)} %copy.84, f32[64,128]{0,1:T(8,128)S(1)} %copy.83, f32[64,128]{0,1:T(8,128)S(1)} %copy.82, f32[64,128]{0,1:T(8,128)S(1)} %copy.81, f32[64,128]{0,1:T(8,128)S(1)} %copy.80), kind=kOutput, calls=%fused_computation.4 | convolution fusion | flops 55574528 | bytes 720896 | tf_op jit(solution)/shard_map/tsm,ksm->ktm/dot_general | solution.py:157
  106.9 29.0 %fusion.58 = f32[1,8,64,128]{2,1,3,0:T(8,128)S(1)} fusion(f32[128,8,64]{2,1,0:T(8,128)S(1)} %fusion.2, f32[8,64,128]{1,0,2:T(8,128)S(1)} %copy.86, f32[64,128]{0,1:T(8,128)S(1)} %copy.85, f32[64,128]{0,1:T(8,128)S(1)} %copy.84, f32[64,128]{0,1:T(8,128)S(1)} %copy.83, f32[64,128]{0,1:T(8,128)S(1)} %copy.82, f32[64,128]{0,1:T(8,128)S(1)} %copy.81, ...), kind=kOutput, calls=%fused_computation.50 | convolution fusion | flops 55640064 | bytes 983040 | tf_op jit(solution)/shard_map/tsm,ksm->ktm/dot_general | solution.py:160
  135.9 29.0 %fusion.52 = f32[1,8,64,128]{2,1,3,0:T(8,128)S(1)} fusion(f32[128,8,64]{2,1,0:T(8,128)S(1)} %fusion.4, f32[8,64,128]{1,0,2:T(8,128)S(1)} %copy.87, f32[64,128]{0,1:T(8,128)S(1)} %copy.85, f32[64,128]{0,1:T(8,128)S(1)} %copy.84, f32[64,128]{0,1:T(8,128)S(1)} %copy.83, f32[64,128]{0,1:T(8,128)S(1)} %copy.82, f32[64,128]{0,1:T(8,128)S(1)} %copy.81, ...), kind=kOutput, calls=%fused_computation.48 | convolution fusion | flops 55640064 | bytes 983040 | tf_op jit(solution)/shard_map/tsm,ksm->ktm/dot_general | solution.py:157
  164.9 0.1 maximum_multiply_fusion
  165.0 0.1 multiply_subtract_fusion
  165.1 0.1 pad_maximum_fusion
  165.2 1.1 copy.92
  166.4 0.1 mul.2693
  166.5 0.1 mul.2687
  166.7 0.1 mul.2729
  166.8 0.1 mul.2723
  166.9 0.5 fusion.139
  167.4 0.6 fusion.137
  168.0 22.1 %all-gather.3.cloned.1.call-done = f32[8,8,64,128]{3,2,1,0:T(8,128)} async-done(((f32[2,8,64,128]{3,2,1,0:T(8,128)}), f32[8,8,64,128]{3,2,1,0:T(8,128)}) %all-gather.3.cloned.1.call-update) | async-done | bytes 2097168 | tf_op jit(solution)/shard_map/all_gather | solution.py:239
  190.2 1.8 reduce_sum.48
  192.0 0.6 convolution_bitcast_fusion.1
  192.6 0.1 multiply_subtract_fusion.2
  192.7 0.2 copy.97
  192.9 0.2 copy.96
  193.2 0.1 maximum_reduce_fusion
  193.3 1.0 convolution_bitcast_fusion
  194.3 0.1 fusion.206
  194.4 0.2 copy.100
  194.5 0.2 copy.99
  194.8 0.8 pad_maximum_fusion.1
  (48 shorter events, 1.5 us)
Async XLA Ops:
  6.5 15.2 %copy-start = (f32[2,8,64,128]{3,2,1,0:T(8,128)S(1)}, f32[2,8,64,128]{3,2,1,0:T(8,128)}, u32[]{:S(2)}) copy-start(f32[2,8,64,128]{3,2,1,0:T(8,128)} %param.3) | copy-start | bytes 1572868
  6.5 7.2 %copy-start.1 = (s32[64]{0:T(128)S(1)}, s32[64]{0:T(128)}, u32[]{:S(2)}) copy-start(s32[64]{0:T(128)} %param.5) | copy-start | bytes 772
  6.5 183.6 %all-gather.3.cloned.1.call-start = ((), (), s32[]{:S(2)}) async-start(), calls=%async_computation | async-start | bytes 2621440 | tf_op jit(solution)/shard_map/all_gather | solution.py:239
  6.5 15.2 %collective-permute-start = (f32[1,2,8,64,128]{4,3,2,1,0:T(8,128)}, f32[1,2,8,64,128]{4,3,2,1,0:T(8,128)S(1)}, u32[]{:S(2)}, u32[]{:S(2)}) collective-permute-start(f32[1,2,8,64,128]{4,3,2,1,0:T(8,128)} %bitcast.160), channel_id=1, source_target_pairs={{0,1},{1,0},{2,3},{3,2},{4,5},{5,4},{6,7},{7,6},{8,9},{9,8},{10,11... | collective-permute-start | bytes 1572872 | tf_op jit(solution)/shard_map/ppermute | solution.py:18
  21.9 24.4 %collective-permute-start.1 = (f32[2,2,8,64,128]{4,3,2,1,0:T(8,128)S(1)}, f32[2,2,8,64,128]{4,3,2,1,0:T(8,128)S(1)}, u32[]{:S(2)}, u32[]{:S(2)}) collective-permute-start(f32[2,2,8,64,128]{4,3,2,1,0:T(8,128)S(1)} %maximum_select_fusion.1), channel_id=1, source_target_pairs={{0,2},{2,0},{1,3},{3,1},{4,6},{6,4},{5,7},{7,5},{8,10},{10,8},{9,1... | collective-permute-start | bytes 3145736 | tf_op jit(solution)/shard_map/ppermute | solution.py:18
Sparse Core Ops, SparseCore 0:
  166.5 23.6 all-gather.2
